TPU v7x, 32 devices: a whole 2x2x4 slice. The times are simulated.
32 devices in a mesh: space: 16 (over z, x, core), traj: 2 (over y).
Axes of the slice: x: 2, y: 2, z: 4, core: 2. Of those that a mesh axis runs over, the one named last changes fastest.
Arguments:
- primal_init: float32 [32, 64, 96, 128], P('traj', 'space'), may hold values from -6 to 6
- adjoint_init: float32 [32, 64, 96, 128], P('traj', 'space'), may hold values from -6 to 6
- diffusion: float32 [3, 64, 96, 128], P(None, 'space'), may hold values from 0.03 to 0.15
- velocity: float32 [3, 64, 96, 128], P(None, 'space'), may hold values from -0.12 to 0.12
- sources: int32 [2, 32], P(None, 'traj'), may hold values from 0 to 786431
Outputs:
- gram: float32 [32, 32], P(None, 'traj')
All inputs are finite; a program needn't handle non-finite values.
Results may differ from a plain program's by a relative error of at most 0.0003.
Values sent between devices are 32-bit elements; how exact they have to be, the bound alone decides.
A program may use at most 128 MiB of HBM per device.

v0:
```python
import functools
import math

import jax
import jax.numpy as jnp
from jax import lax
from jax.experimental import pallas as pl
from jax.experimental.pallas import tpu as pltpu
from jax.sharding import PartitionSpec as P

STEPS = 4
IMPULSE = 1024
GROUP = 1
CHUNKS = 2
MESH = pl.DeviceIdType.MESH


def coefficients(dv, coef, zz):
    rows, lanes = coef.shape[2:]
    row = lax.broadcasted_iota(jnp.int32, (rows, lanes), 0)
    lane = lax.broadcasted_iota(jnp.int32, (rows, lanes), 1)

    def faces(component, plane):
        d, v = dv[0, component, plane], dv[1, component, plane]
        return d + 0.5 * v, d - 0.5 * v

    out_z, in_z = faces(0, zz + 1)
    out_z_below, in_z_below = faces(0, zz)
    out_x, in_x = faces(1, zz + 1)
    out_y, in_y = faces(2, zz + 1)
    zero = jnp.zeros((rows, lanes), jnp.float32)
    below_x = lambda value: jnp.where(row == 0, zero, pltpu.roll(value, 1, 0))
    below_y = lambda value: jnp.where(lane == 0, zero, pltpu.roll(value, 1, 1))
    centre = out_z + in_z_below + out_x + below_x(in_x) + out_y + below_y(in_y)
    coef[0, zz] = 1.0 - centre
    coef[1, zz] = in_z
    coef[2, zz] = out_z_below
    coef[3, zz] = jnp.where(row == rows - 1, zero, in_x)
    coef[4, zz] = below_x(out_x)
    coef[5, zz] = jnp.where(lane == lanes - 1, zero, in_y)
    coef[6, zz] = below_y(out_y)


def kernel(
    dims,
    src_ref,
    p_ref,
    a_ref,
    d_ref,
    v_ref,
    out_ref,
    cur,
    a_all,
    dv,
    coef,
    gred,
    part,
    part2,
    local_sem,
    coef_send,
    coef_recv,
    below_send,
    below_recv,
    a_send,
    a_recv,
    up_send,
    up_recv,
    down_send,
    down_recv,
    red_send,
    red_recv,
    red2_send,
    red2_recv,
):
    n, n_traj, quad, chunks = dims
    fields, planes, rows, lanes = p_ref.shape
    size = fields // chunks
    steps = 2 * STEPS
    me = lax.axis_index("space")
    my_traj = lax.axis_index("traj")
    has_up, has_down = me < n - 1, me > 0

    barrier = pltpu.get_barrier_semaphore()

    @pl.loop(1, n)
    def _(ahead):
        pl.semaphore_signal(
            barrier, inc=1, device_id={"space": lax.rem(me + ahead, n)}, device_id_type=MESH
        )

    for ahead in range(1, n_traj):
        pl.semaphore_signal(
            barrier,
            inc=1,
            device_id={"traj": lax.rem(my_traj + ahead, n_traj)},
            device_id_type=MESH,
        )
    pl.semaphore_wait(barrier, n - 1 + n_traj - 1)

    local = [
        pltpu.make_async_copy(ref, dv.at[i, :, pl.ds(1, planes)], local_sem.at[i])
        for i, ref in enumerate((d_ref, v_ref))
    ]
    for copy in local:
        copy.start()

    def below(i, ref):
        return pltpu.make_async_remote_copy(
            src_ref=ref.at[0, planes - 1],
            dst_ref=dv.at[i, 0, 0],
            send_sem=below_send.at[i],
            recv_sem=below_recv.at[i],
            device_id={"space": jnp.minimum(me + 1, n - 1)},
            device_id_type=MESH,
        )

    @pl.when(has_up)
    def _():
        for i, ref in enumerate((d_ref, v_ref)):
            below(i, ref).start()

    grid = (rows, lanes)
    offset = lax.broadcasted_iota(jnp.int32, grid, 0) * lanes + lax.broadcasted_iota(
        jnp.int32, grid, 1
    )

    def halo_up(slot, chunk):
        which = pl.ds(chunk * size, size)
        return pltpu.make_async_remote_copy(
            src_ref=cur.at[slot, which, planes],
            dst_ref=cur.at[slot, which, 0],
            send_sem=up_send.at[slot, chunk],
            recv_sem=up_recv.at[slot, chunk],
            device_id={"space": jnp.minimum(me + 1, n - 1)},
            device_id_type=MESH,
        )

    def halo_down(slot, chunk):
        which = pl.ds(chunk * size, size)
        return pltpu.make_async_remote_copy(
            src_ref=cur.at[slot, which, 1],
            dst_ref=cur.at[slot, which, planes + 1],
            send_sem=down_send.at[slot, chunk],
            recv_sem=down_recv.at[slot, chunk],
            device_id={"space": jnp.maximum(me - 1, 0)},
            device_id_type=MESH,
        )

    def send_halos(slot, chunk):
        @pl.when(has_up)
        def _():
            halo_up(slot, chunk).start()

        @pl.when(has_down)
        def _():
            halo_down(slot, chunk).start()

    def wait_sent(slot, chunk):
        @pl.when(has_up)
        def _():
            halo_up(slot, chunk).wait_send()

        @pl.when(has_down)
        def _():
            halo_down(slot, chunk).wait_send()

    def wait_halos(slot, chunk):
        @pl.when(has_down)
        def _():
            halo_up(slot, chunk).wait_recv()

        @pl.when(has_up)
        def _():
            halo_down(slot, chunk).wait_recv()

    for chunk in range(chunks):

        @pl.loop(chunk * size, (chunk + 1) * size)
        def _(f):
            source = src_ref[0, f]
            for zz in range(planes):
                cell = offset + (me * planes + zz) * (rows * lanes)
                cur[0, f, zz + 1] = p_ref[f, zz] + jnp.where(cell == source, float(IMPULSE), 0.0)

        send_halos(0, chunk)

    @pl.loop(0, fields)
    def _(f):
        source = src_ref[1, f]
        for zz in range(planes):
            cell = offset + (me * planes + zz) * (rows * lanes)
            a_all[my_traj, f, zz] = a_ref[f, zz] + jnp.where(cell == source, float(IMPULSE), 0.0)

    def gather(ahead):
        return pltpu.make_async_remote_copy(
            src_ref=a_all.at[my_traj],
            dst_ref=a_all.at[my_traj],
            send_sem=a_send.at[ahead - 1],
            recv_sem=a_recv.at[ahead - 1],
            device_id={"traj": lax.rem(my_traj + ahead, n_traj)},
            device_id_type=MESH,
        )

    for ahead in range(1, n_traj):
        gather(ahead).start()

    @pl.when(me == 0)
    def _():
        dv[:, 0, 0] = jnp.zeros((2, rows, lanes), jnp.float32)

        @pl.loop(0, fields)
        def _(f):
            for slot in range(2):
                cur[slot, f, 0] = jnp.zeros(grid, jnp.float32)

    @pl.when(me == n - 1)
    def _():
        @pl.loop(0, fields)
        def _(f):
            for slot in range(2):
                cur[slot, f, planes + 1] = jnp.zeros(grid, jnp.float32)

    for copy in local:
        copy.wait()

    @pl.when(has_down)
    def _():
        for i, ref in enumerate((d_ref, v_ref)):
            below(i, ref).wait_recv()

    @pl.loop(0, planes)
    def _(zz):
        coefficients(dv, coef, zz)

    def update(slot, f, zz):
        p = cur[slot, f, zz + 1]
        cur[1 - slot, f, zz + 1] = (
            coef[0, zz] * p
            + coef[1, zz] * cur[slot, f, zz + 2]
            + coef[2, zz] * cur[slot, f, zz]
            + coef[3, zz] * pltpu.roll(p, rows - 1, 0)
            + coef[4, zz] * pltpu.roll(p, 1, 0)
            + coef[5, zz] * pltpu.roll(p, lanes - 1, 1)
            + coef[6, zz] * pltpu.roll(p, 1, 1)
        )

    def outer_planes(slot, chunk):
        @pl.loop(chunk * size, (chunk + 1) * size)
        def _(f):
            for zz in (0, planes - 1):
                update(slot, f, zz)

    def inner_planes(slot, chunk):
        @pl.loop(chunk * size, (chunk + 1) * size)
        def _(f):
            for zz in range(1, planes - 1):
                update(slot, f, zz)

    @pl.loop(0, steps - 1)
    def _(t):
        slot = lax.rem(t, 2)
        for chunk in range(chunks):

            @pl.when(t > 0)
            def _():
                wait_sent(1 - slot, chunk)

            wait_halos(slot, chunk)
            outer_planes(slot, chunk)
            send_halos(1 - slot, chunk)
            inner_planes(slot, chunk)

    side = math.gcd(4, size)
    total = n_traj * fields

    def gram_of(chunk):
        tiles = rows // 8

        @pl.loop(0, total // 4)
        def _(kb):
            owner, k0 = lax.div(kb * 4, fields), lax.rem(kb * 4, fields)

            @pl.loop(0, size // side)
            def _(jb):
                j0 = chunk * size + jb * side

                def tile(i, sums):
                    zz, start = lax.div(i, tiles), pl.multiple_of(lax.rem(i, tiles) * 8, 8)
                    left = [a_all[owner, k0 + k, zz, pl.ds(start, 8)] for k in range(4)]
                    right = [cur[0, j0 + j, zz + 1, pl.ds(start, 8)] for j in range(side)]
                    return tuple(
                        sums[k * side + j] + left[k] * right[j]
                        for k in range(4)
                        for j in range(side)
                    )

                zero = jnp.zeros((8, lanes), jnp.float32)
                sums = lax.fori_loop(0, planes * tiles, tile, (zero,) * (4 * side), unroll=4)
                for k in range(4):
                    for j in range(side):
                        gred[kb * 4 + k, pl.ds(j0 + j, 1)] = jnp.sum(
                            sums[k * side + j], axis=0, keepdims=True
                        )

    for chunk in range(chunks):
        wait_sent(0, chunk)
        wait_halos(1, chunk)
        outer_planes(1, chunk)
        inner_planes(1, chunk)
        if chunk == 0:
            for ahead in range(1, n_traj):
                gather(ahead).wait_recv()
        gram_of(chunk)

    for chunk in range(chunks):
        wait_sent(1, chunk)

    groups = n // quad
    mine, place = lax.div(me, quad), lax.rem(me, quad)
    part[place] = jnp.sum(gred[...], axis=-1)

    def inside(ahead):
        return pltpu.make_async_remote_copy(
            src_ref=part.at[place],
            dst_ref=part.at[place],
            send_sem=red_send.at[ahead - 1],
            recv_sem=red_recv.at[ahead - 1],
            device_id={"space": mine * quad + lax.rem(place + ahead, quad)},
            device_id_type=MESH,
        )

    for ahead in range(1, quad):
        inside(ahead).start()
    for ahead in range(1, quad):
        inside(ahead).wait_recv()
    value = part[0]
    for i in range(1, quad):
        value = value + part[i]
    part2[mine] = value

    def across(ahead):
        return pltpu.make_async_remote_copy(
            src_ref=part2.at[mine],
            dst_ref=part2.at[mine],
            send_sem=red2_send.at[ahead - 1],
            recv_sem=red2_recv.at[ahead - 1],
            device_id={"space": lax.rem(mine + ahead, groups) * quad + place},
            device_id_type=MESH,
        )

    for ahead in range(1, groups):
        across(ahead).start()
    for ahead in range(1, groups):
        across(ahead).wait_recv()
    value = part2[0]
    for i in range(1, groups):
        value = value + part2[i]
    out_ref[...] = value / math.sqrt(n * planes * rows * lanes)

    for ahead in range(1, quad):
        inside(ahead).wait_send()
    for ahead in range(1, groups):
        across(ahead).wait_send()
    for ahead in range(1, n_traj):
        gather(ahead).wait_send()

    @pl.when(has_up)
    def _():
        for i, ref in enumerate((d_ref, v_ref)):
            below(i, ref).wait_send()


def solution(mesh):
    n, n_traj = mesh.shape["space"], mesh.shape["traj"]

    def on_device(primal_init, adjoint_init, diffusion, velocity, sources):
        fields, planes, rows, lanes = primal_init.shape
        quad = math.gcd(4, n)
        chunks = math.gcd(CHUNKS, fields)
        total = n_traj * fields
        vmem = pl.BlockSpec(memory_space=pltpu.VMEM)
        dma = pltpu.SemaphoreType.DMA
        f32 = jnp.float32
        return pl.pallas_call(
            functools.partial(kernel, (n, n_traj, quad, chunks)),
            out_shape=jax.ShapeDtypeStruct((total, fields), f32),
            in_specs=[pl.BlockSpec(memory_space=pltpu.SMEM)] + [vmem] * 4,
            out_specs=vmem,
            scratch_shapes=[
                pltpu.VMEM((2, fields, planes + 2, rows, lanes), f32),
                pltpu.VMEM((n_traj, fields, planes, rows, lanes), f32),
                pltpu.VMEM((2, 3, planes + 1, rows, lanes), f32),
                pltpu.VMEM((7, planes, rows, lanes), f32),
                pltpu.VMEM((total, fields, lanes), f32),
                pltpu.VMEM((quad, total, fields), f32),
                pltpu.VMEM((n // quad, total, fields), f32),
                dma((2,)),
                dma((2,)),
                dma((2,)),
                dma((2,)),
                dma((2,)),
                dma((max(1, n_traj - 1),)),
                dma((max(1, n_traj - 1),)),
                dma((2, chunks)),
                dma((2, chunks)),
                dma((2, chunks)),
                dma((2, chunks)),
                dma((max(1, quad - 1),)),
                dma((max(1, quad - 1),)),
                dma((max(1, n // quad - 1),)),
                dma((max(1, n // quad - 1),)),
            ],
            compiler_params=pltpu.CompilerParams(
                collective_id=0, has_side_effects=True, vmem_limit_bytes=48 << 20
            ),
        )(sources, primal_init, adjoint_init, diffusion, velocity)

    return jax.shard_map(
        on_device,
        mesh=mesh,
        in_specs=(
            P("traj", "space", None, None),
            P("traj", "space", None, None),
            P(None, "space", None, None),
            P(None, "space", None, None),
            P(None, "traj"),
        ),
        out_specs=P(None, "traj"),
        check_vma=False,
    )
```

profile of v0, /device:TPU:0, one launch (start us, length us, event | category | flops | bytes accessed | tf_op | source)
XLA Modules:
  0.0 170.4 jit_solution(8463273816419585734)
XLA Ops:
  0.0 0.0 copy-start
  0.0 1.9 %copy-done = f32[16,4,96,128]{3,2,1,0:T(8,128)S(1)} copy-done((f32[16,4,96,128]{3,2,1,0:T(8,128)S(1)}, f32[16,4,96,128]{3,2,1,0:T(8,128)}, u32[]{:S(2)}) %copy-start) | copy-done | bytes 3145752
  1.9 0.0 copy-start.1
  1.9 1.1 copy-done.1
  3.0 0.0 copy-start.2
  3.0 1.1 copy-done.2
  4.0 0.0 copy-start.3
  4.0 0.7 copy-done.3
  4.7 165.0 %shard_map.55 = f32[32,16]{1,0:T(8,128)S(1)} custom-call(s32[2,16]{1,0:T(2,128)S(1)} %copy-done.3, f32[16,4,96,128]{3,2,1,0:T(8,128)S(1)} %copy-done, f32[16,4,96,128]{3,2,1,0:T(8,128)} %a_ref.1, f32[3,4,96,128]{3,2,1,0:T(8,128)S(1)} %copy-done.1, f32[3,4,96,128]{3,2,1,0:T(8,128)S(1)} %copy-done.2), custom_call_target="tpu_custom_call" | custom-call | tf_op jit(solution)/shard_map/pallas_call | solution.py:384
  169.7 0.7 copy.6
Async XLA Ops:
  0.0 1.9 %copy-start = (f32[16,4,96,128]{3,2,1,0:T(8,128)S(1)}, f32[16,4,96,128]{3,2,1,0:T(8,128)}, u32[]{:S(2)}) copy-start(f32[16,4,96,128]{3,2,1,0:T(8,128)} %p_ref.1) | copy-start | bytes 9437188
  1.9 1.1 copy-start.1
  3.0 1.1 copy-start.2
  4.0 0.7 copy-start.3
where the time goes:
time: 171 us; the launch traced here: 170 us
  Pallas kernels  165 us (96%)
  local copies, waits for them, and re-layouts  5.36 us (3%)
    pallas_call x1, Pallas kernels, on_device(): pl.pallas_call(functools.partial(kernel, (n, n_traj, quad, chunks)), out_...  165 us
    unnamed x8, local copies, waits for them, and re-layouts  4.69 us

commit v1 on v0

v1 whole, which is shorter than its diff:
```python
import functools
import math

import jax
import jax.numpy as jnp
from jax import lax
from jax.experimental import pallas as pl
from jax.experimental.pallas import tpu as pltpu
from jax.sharding import PartitionSpec as P

STEPS = 4
IMPULSE = 1024
GROUP = 4
LAG = 3
MESH = pl.DeviceIdType.MESH


def coefficients(dv, coef, zz):
    rows, lanes = coef.shape[2:]
    row = lax.broadcasted_iota(jnp.int32, (rows, lanes), 0)
    lane = lax.broadcasted_iota(jnp.int32, (rows, lanes), 1)

    def faces(component, plane):
        d, v = dv[0, component, plane], dv[1, component, plane]
        return d + 0.5 * v, d - 0.5 * v

    out_z, in_z = faces(0, zz + 1)
    out_z_below, in_z_below = faces(0, zz)
    out_x, in_x = faces(1, zz + 1)
    out_y, in_y = faces(2, zz + 1)
    zero = jnp.zeros((rows, lanes), jnp.float32)
    below_x = lambda value: jnp.where(row == 0, zero, pltpu.roll(value, 1, 0))
    below_y = lambda value: jnp.where(lane == 0, zero, pltpu.roll(value, 1, 1))
    centre = out_z + in_z_below + out_x + below_x(in_x) + out_y + below_y(in_y)
    coef[0, zz] = 1.0 - centre
    coef[1, zz] = in_z
    coef[2, zz] = out_z_below
    coef[3, zz] = jnp.where(row == rows - 1, zero, in_x)
    coef[4, zz] = below_x(out_x)
    coef[5, zz] = jnp.where(lane == lanes - 1, zero, in_y)
    coef[6, zz] = below_y(out_y)


def kernel(
    dims,
    src_ref,
    p_ref,
    a_ref,
    d_ref,
    v_ref,
    out_ref,
    start,
    cur,
    final,
    a_all,
    dv,
    coef,
    gred,
    part,
    part2,
    local_sem,
    chip_send,
    chip_recv,
    far_send,
    far_recv,
    relay_send,
    relay_recv,
    below_send,
    below_recv,
    a_send,
    a_recv,
    in_send,
    in_recv,
    back_send,
    back_recv,
    up_send,
    up_recv,
    down_send,
    down_recv,
    red_send,
    red_recv,
    red2_send,
    red2_recv,
):
    n, n_traj, quad = dims
    fields, planes, rows, lanes = p_ref.shape
    held = fields // quad
    deep = planes * quad
    steps = 2 * STEPS
    me = lax.axis_index("space")
    my_traj = lax.axis_index("traj")
    groups = n // quad
    mine, place = lax.div(me, quad), lax.rem(me, quad)
    beside = place + 1 - 2 * lax.rem(place, 2)
    far = lax.rem(place + 2, quad)
    has_up, has_down = mine < groups - 1, mine > 0
    above_id = {"space": jnp.minimum(me + quad, n - quad + place)}
    below_id = {"space": jnp.maximum(me - quad, place)}

    barrier = pltpu.get_barrier_semaphore()

    @pl.loop(1, n)
    def _(ahead):
        pl.semaphore_signal(
            barrier, inc=1, device_id={"space": lax.rem(me + ahead, n)}, device_id_type=MESH
        )

    for ahead in range(1, n_traj):
        pl.semaphore_signal(
            barrier,
            inc=1,
            device_id={"traj": lax.rem(my_traj + ahead, n_traj)},
            device_id_type=MESH,
        )
    pl.semaphore_wait(barrier, n - 1 + n_traj - 1)

    pair = (d_ref, v_ref)

    def faces_at(i, piece):
        return dv.at[i, :, pl.ds(1 + planes * piece, planes)]

    def send_far(i):
        return pltpu.make_async_remote_copy(
            src_ref=pair[i],
            dst_ref=faces_at(i, place),
            send_sem=far_send.at[i],
            recv_sem=far_recv.at[i],
            device_id={"space": mine * quad + far},
            device_id_type=MESH,
        )

    def send_beside(i):
        return pltpu.make_async_remote_copy(
            src_ref=pair[i],
            dst_ref=faces_at(i, place),
            send_sem=chip_send.at[i],
            recv_sem=chip_recv.at[i],
            device_id={"space": mine * quad + beside},
            device_id_type=MESH,
        )

    def relay(i):
        return pltpu.make_async_remote_copy(
            src_ref=faces_at(i, far),
            dst_ref=faces_at(i, far),
            send_sem=relay_send.at[i],
            recv_sem=relay_recv.at[i],
            device_id={"space": mine * quad + beside},
            device_id_type=MESH,
        )

    local = [
        pltpu.make_async_copy(pair[i], faces_at(i, place), local_sem.at[i]) for i in range(2)
    ]
    for i in range(2):
        send_far(i).start()
    for i in range(2):
        send_beside(i).start()
        local[i].start()

    grid = (rows, lanes)
    offset = lax.broadcasted_iota(jnp.int32, grid, 0) * lanes + lax.broadcasted_iota(
        jnp.int32, grid, 1
    )

    def with_impulse(value, source, zz):
        cell = offset + (me * planes + zz) * (rows * lanes)
        return value + jnp.where(cell == source, float(IMPULSE), 0.0)

    def hand_over(c, ahead):
        target = lax.rem(place + ahead, quad)
        return pltpu.make_async_remote_copy(
            src_ref=start.at[target * held + c],
            dst_ref=cur.at[0, c, pl.ds(1 + planes * place, planes)],
            send_sem=in_send.at[c, ahead - 1],
            recv_sem=in_recv.at[c, ahead - 1],
            device_id={"space": mine * quad + target},
            device_id_type=MESH,
        )

    def hand_back(c, ahead):
        target = lax.rem(place + ahead, quad)
        return pltpu.make_async_remote_copy(
            src_ref=cur.at[0, c, pl.ds(1 + planes * target, planes)],
            dst_ref=final.at[place * held + c],
            send_sem=back_send.at[c, ahead - 1],
            recv_sem=back_recv.at[c, ahead - 1],
            device_id={"space": mine * quad + target},
            device_id_type=MESH,
        )

    @pl.loop(0, held)
    def _(c):
        for owner in range(quad):
            f = owner * held + c
            for zz in range(planes):
                start[f, zz] = with_impulse(p_ref[f, zz], src_ref[0, f], zz)
        for ahead in (2, 1, 3):
            hand_over(c, ahead).start()
        for zz in range(planes):
            cur[0, c, 1 + planes * place + zz] = start[place * held + c, zz]

    @pl.loop(0, fields)
    def _(f):
        for zz in range(planes):
            a_all[my_traj, f, zz] = with_impulse(a_ref[f, zz], src_ref[1, f], zz)

    def gather(ahead):
        return pltpu.make_async_remote_copy(
            src_ref=a_all.at[my_traj],
            dst_ref=a_all.at[my_traj],
            send_sem=a_send.at[ahead - 1],
            recv_sem=a_recv.at[ahead - 1],
            device_id={"traj": lax.rem(my_traj + ahead, n_traj)},
            device_id_type=MESH,
        )

    for ahead in range(1, n_traj):
        gather(ahead).start()

    @pl.when(mine == 0)
    def _():
        for i in range(2):
            dv[i, 0, 0] = jnp.zeros(grid, jnp.float32)

        @pl.loop(0, held)
        def _(c):
            for slot in range(2):
                cur[slot, c, 0] = jnp.zeros(grid, jnp.float32)

    @pl.when(mine == groups - 1)
    def _():
        @pl.loop(0, held)
        def _(c):
            for slot in range(2):
                cur[slot, c, deep + 1] = jnp.zeros(grid, jnp.float32)

    for i in range(2):
        send_far(i).wait_recv()
        relay(i).start()
    for i in range(2):
        local[i].wait()
        send_beside(i).wait_recv()
        relay(i).wait_recv()

    def below(i):
        return pltpu.make_async_remote_copy(
            src_ref=dv.at[i, 0, deep],
            dst_ref=dv.at[i, 0, 0],
            send_sem=below_send.at[i],
            recv_sem=below_recv.at[i],
            device_id=above_id,
            device_id_type=MESH,
        )

    @pl.when(has_up)
    def _():
        for i in range(2):
            below(i).start()

    @pl.loop(1, deep)
    def _(zz):
        coefficients(dv, coef, zz)

    @pl.when(has_down)
    def _():
        for i in range(2):
            below(i).wait_recv()

    coefficients(dv, coef, 0)

    def halo_up(slot, c):
        return pltpu.make_async_remote_copy(
            src_ref=cur.at[slot, c, deep],
            dst_ref=cur.at[slot, c, 0],
            send_sem=up_send.at[slot, c],
            recv_sem=up_recv.at[slot, c],
            device_id=above_id,
            device_id_type=MESH,
        )

    def halo_down(slot, c):
        return pltpu.make_async_remote_copy(
            src_ref=cur.at[slot, c, 1],
            dst_ref=cur.at[slot, c, deep + 1],
            send_sem=down_send.at[slot, c],
            recv_sem=down_recv.at[slot, c],
            device_id=below_id,
            device_id_type=MESH,
        )

    def send_halos(slot, c):
        @pl.when(has_up)
        def _():
            halo_up(slot, c).start()

        @pl.when(has_down)
        def _():
            halo_down(slot, c).start()

    def wait_sent(slot, c):
        @pl.when(has_up)
        def _():
            halo_up(slot, c).wait_send()

        @pl.when(has_down)
        def _():
            halo_down(slot, c).wait_send()

    def wait_halos(slot, c):
        @pl.when(has_down)
        def _():
            halo_up(slot, c).wait_recv()

        @pl.when(has_up)
        def _():
            halo_down(slot, c).wait_recv()

    def update(slot, c, zz):
        p = cur[slot, c, zz + 1]
        cur[1 - slot, c, zz + 1] = (
            coef[0, zz] * p
            + coef[1, zz] * cur[slot, c, zz + 2]
            + coef[2, zz] * cur[slot, c, zz]
            + coef[3, zz] * pltpu.roll(p, rows - 1, 0)
            + coef[4, zz] * pltpu.roll(p, 1, 0)
            + coef[5, zz] * pltpu.roll(p, lanes - 1, 1)
            + coef[6, zz] * pltpu.roll(p, 1, 1)
        )

    @pl.loop(0, steps + 1 + (held - 1) * LAG)
    def _(turn):
        @pl.loop(0, held)
        def _(c):
            t = turn - c * LAG - 1

            @pl.when(t == -1)
            def _():
                for ahead in range(1, quad):
                    hand_over(c, ahead).wait_recv()
                send_halos(0, c)

            @pl.when((t >= 0) & (t < steps))
            def _():
                slot = lax.rem(t, 2)

                @pl.when(t > 0)
                def _():
                    wait_sent(1 - slot, c)

                wait_halos(slot, c)
                update(slot, c, 0)
                update(slot, c, deep - 1)

                @pl.when(t < steps - 1)
                def _():
                    send_halos(1 - slot, c)

                @pl.loop(1, deep - 1)
                def _(zz):
                    update(slot, c, zz)

            @pl.when(t == steps - 1)
            def _():
                for ahead in (2, 1, 3):
                    hand_back(c, ahead).start()
                for zz in range(planes):
                    final[place * held + c, zz] = cur[0, c, 1 + planes * place + zz]

    def gram_of(c, owner):
        tiles = rows // 8

        @pl.loop(0, fields // 4)
        def _(kb):
            def tile(i, sums):
                zz, first = lax.div(i, tiles), pl.multiple_of(lax.rem(i, tiles) * 8, 8)
                left = [a_all[owner, kb * 4 + k, zz, pl.ds(first, 8)] for k in range(4)]
                right = [final[j * held + c, zz, pl.ds(first, 8)] for j in range(quad)]
                return tuple(
                    sums[k * quad + j] + left[k] * right[j] for k in range(4) for j in range(quad)
                )

            zero = jnp.zeros((8, lanes), jnp.float32)
            sums = lax.fori_loop(0, planes * tiles, tile, (zero,) * (4 * quad), unroll=4)
            for k in range(4):
                for j in range(quad):
                    gred[owner * fields + kb * 4 + k, pl.ds(j * held + c, 1)] = jnp.sum(
                        sums[k * quad + j], axis=0, keepdims=True
                    )

    for ahead in range(1, n_traj):
        gather(ahead).wait_recv()

    @pl.loop(0, held)
    def _(c):
        for ahead in range(1, quad):
            hand_back(c, ahead).wait_recv()

        @pl.loop(0, n_traj)
        def _(owner):
            gram_of(c, owner)

    @pl.loop(0, held)
    def _(c):
        wait_sent(1, c)
        for ahead in range(1, quad):
            hand_over(c, ahead).wait_send()
            hand_back(c, ahead).wait_send()

    part[place] = jnp.sum(gred[...], axis=-1)

    def inside(ahead):
        return pltpu.make_async_remote_copy(
            src_ref=part.at[place],
            dst_ref=part.at[place],
            send_sem=red_send.at[ahead - 1],
            recv_sem=red_recv.at[ahead - 1],
            device_id={"space": mine * quad + lax.rem(place + ahead, quad)},
            device_id_type=MESH,
        )

    for ahead in range(1, quad):
        inside(ahead).start()
    for ahead in range(1, quad):
        inside(ahead).wait_recv()
    value = part[0]
    for i in range(1, quad):
        value = value + part[i]
    part2[mine] = value

    def across(ahead):
        return pltpu.make_async_remote_copy(
            src_ref=part2.at[mine],
            dst_ref=part2.at[mine],
            send_sem=red2_send.at[ahead - 1],
            recv_sem=red2_recv.at[ahead - 1],
            device_id={"space": lax.rem(mine + ahead, groups) * quad + place},
            device_id_type=MESH,
        )

    for ahead in range(1, groups):
        across(ahead).start()
    for ahead in range(1, groups):
        across(ahead).wait_recv()
    value = part2[0]
    for i in range(1, groups):
        value = value + part2[i]
    out_ref[...] = value / math.sqrt(n * planes * rows * lanes)

    for ahead in range(1, quad):
        inside(ahead).wait_send()
    for ahead in range(1, groups):
        across(ahead).wait_send()
    for ahead in range(1, n_traj):
        gather(ahead).wait_send()

    for i in range(2):
        send_far(i).wait_send()
        send_beside(i).wait_send()
        relay(i).wait_send()

    @pl.when(has_up)
    def _():
        for i in range(2):
            below(i).wait_send()


def solution(mesh):
    n, n_traj = mesh.shape["space"], mesh.shape["traj"]

    def on_device(primal_init, adjoint_init, diffusion, velocity, sources):
        fields, planes, rows, lanes = primal_init.shape
        quad = GROUP
        assert n % quad == 0 and fields % quad == 0
        held, deep = fields // quad, planes * quad
        total = n_traj * fields
        vmem = pl.BlockSpec(memory_space=pltpu.VMEM)
        dma = pltpu.SemaphoreType.DMA
        f32 = jnp.float32
        return pl.pallas_call(
            functools.partial(kernel, (n, n_traj, quad)),
            out_shape=jax.ShapeDtypeStruct((total, fields), f32),
            in_specs=[pl.BlockSpec(memory_space=pltpu.SMEM)] + [vmem] * 4,
            out_specs=vmem,
            scratch_shapes=[
                pltpu.VMEM((fields, planes, rows, lanes), f32),
                pltpu.VMEM((2, held, deep + 2, rows, lanes), f32),
                pltpu.VMEM((fields, planes, rows, lanes), f32),
                pltpu.VMEM((n_traj, fields, planes, rows, lanes), f32),
                pltpu.VMEM((2, 3, deep + 1, rows, lanes), f32),
                pltpu.VMEM((7, deep, rows, lanes), f32),
                pltpu.VMEM((total, fields, lanes), f32),
                pltpu.VMEM((quad, total, fields), f32),
                pltpu.VMEM((n // quad, total, fields), f32),
                *[dma((2,))] * 9,
                *[dma((max(1, n_traj - 1),))] * 2,
                *[dma((held, quad - 1))] * 4,
                *[dma((2, held))] * 4,
                *[dma((quad - 1,))] * 2,
                *[dma((max(1, n // quad - 1),))] * 2,
            ],
            compiler_params=pltpu.CompilerParams(
                collective_id=0, has_side_effects=True, vmem_limit_bytes=48 << 20
            ),
        )(sources, primal_init, adjoint_init, diffusion, velocity)

    return jax.shard_map(
        on_device,
        mesh=mesh,
        in_specs=(
            P("traj", "space", None, None),
            P("traj", "space", None, None),
            P(None, "space", None, None),
            P(None, "space", None, None),
            P(None, "traj"),
        ),
        out_specs=P(None, "traj"),
        check_vma=False,
    )
```

time: 171 us -> 137 us (0.80)
  Pallas kernels: 165 us -> 131 us
    pallas_call x1, Pallas kernels: 165 us -> 131 us  [on_device(): pl.pallas_call(functools.partial(kernel, (n, n_traj, quad)), out_shape=ja...]
where the time goes in v1:
time: 137 us; the launch traced here: 136 us
  Pallas kernels  131 us (96%)
  local copies, waits for them, and re-layouts  5.36 us (4%)
    pallas_call x1, Pallas kernels, on_device(): pl.pallas_call(functools.partial(kernel, (n, n_traj, quad)), out_shape=ja...  131 us
    unnamed x8, local copies, waits for them, and re-layouts  4.69 us

profile of v1, /device:TPU:0, one launch (start us, length us, event | category | flops | bytes accessed | tf_op | source)
XLA Modules:
  0.0 136.4 jit_solution(6546877401767800668)
XLA Ops:
  0.0 0.0 copy-start
  0.0 1.9 %copy-done = f32[16,4,96,128]{3,2,1,0:T(8,128)S(1)} copy-done((f32[16,4,96,128]{3,2,1,0:T(8,128)S(1)}, f32[16,4,96,128]{3,2,1,0:T(8,128)}, u32[]{:S(2)}) %copy-start) | copy-done | bytes 3145752
  1.9 0.0 copy-start.1
  1.9 1.1 copy-done.1
  3.0 0.0 copy-start.2
  3.0 1.1 copy-done.2
  4.0 0.0 copy-start.3
  4.0 0.7 copy-done.3
  4.7 131.0 %shard_map.55 = f32[32,16]{1,0:T(8,128)S(1)} custom-call(s32[2,16]{1,0:T(2,128)S(1)} %copy-done.3, f32[16,4,96,128]{3,2,1,0:T(8,128)S(1)} %copy-done, f32[16,4,96,128]{3,2,1,0:T(8,128)} %a_ref.1, f32[3,4,96,128]{3,2,1,0:T(8,128)S(1)} %copy-done.1, f32[3,4,96,128]{3,2,1,0:T(8,128)S(1)} %copy-done.2), custom_call_target="tpu_custom_call" | custom-call | tf_op jit(solution)/shard_map/pallas_call | solution.py:480
  135.7 0.7 copy.6
Async XLA Ops:
  0.0 1.9 %copy-start = (f32[16,4,96,128]{3,2,1,0:T(8,128)S(1)}, f32[16,4,96,128]{3,2,1,0:T(8,128)}, u32[]{:S(2)}) copy-start(f32[16,4,96,128]{3,2,1,0:T(8,128)} %p_ref.1) | copy-start | bytes 9437188
  1.9 1.1 copy-start.1
  3.0 1.1 copy-start.2
  4.0 0.7 copy-start.3

commit v2 on v1

--- a/solution.py
+++ b/solution.py
@@ -11,7 +11,7 @@
 STEPS = 4
 IMPULSE = 1024
 GROUP = 4
-LAG = 3
+LAG = 2
 MESH = pl.DeviceIdType.MESH
 
 

time: 137 us -> 132 us (0.964)
  Pallas kernels: 131 us -> 127 us
    pallas_call x1, Pallas kernels: 131 us -> 127 us  [on_device(): pl.pallas_call(functools.partial(kernel, (n, n_traj, quad)), out_shape=ja...]
where the time goes in v2:
time: 132 us
  Pallas kernels  127 us (96%)
  local copies, waits for them, and re-layouts  5.36 us (4%)
    pallas_call x1, Pallas kernels, on_device(): pl.pallas_call(functools.partial(kernel, (n, n_traj, quad)), out_shape=ja...  127 us
    unnamed x8, local copies, waits for them, and re-layouts  4.69 us

profile of v2, /device:TPU:0, one launch (start us, length us, event | category | flops | bytes accessed | tf_op | source)
XLA Modules:
  0.0 131.9 jit_solution(15305475734865677015)
XLA Ops:
  0.0 0.0 copy-start
  0.0 1.9 %copy-done = f32[16,4,96,128]{3,2,1,0:T(8,128)S(1)} copy-done((f32[16,4,96,128]{3,2,1,0:T(8,128)S(1)}, f32[16,4,96,128]{3,2,1,0:T(8,128)}, u32[]{:S(2)}) %copy-start) | copy-done | bytes 3145752
  1.9 0.0 copy-start.1
  1.9 1.1 copy-done.1
  3.0 0.0 copy-start.2
  3.0 1.1 copy-done.2
  4.0 0.0 copy-start.3
  4.0 0.7 copy-done.3
  4.7 126.6 %shard_map.55 = f32[32,16]{1,0:T(8,128)S(1)} custom-call(s32[2,16]{1,0:T(2,128)S(1)} %copy-done.3, f32[16,4,96,128]{3,2,1,0:T(8,128)S(1)} %copy-done, f32[16,4,96,128]{3,2,1,0:T(8,128)} %a_ref.1, f32[3,4,96,128]{3,2,1,0:T(8,128)S(1)} %copy-done.1, f32[3,4,96,128]{3,2,1,0:T(8,128)S(1)} %copy-done.2), custom_call_target="tpu_custom_call" | custom-call | tf_op jit(solution)/shard_map/pallas_call | solution.py:480
  131.3 0.7 copy.6
Async XLA Ops:
  0.0 1.9 %copy-start = (f32[16,4,96,128]{3,2,1,0:T(8,128)S(1)}, f32[16,4,96,128]{3,2,1,0:T(8,128)}, u32[]{:S(2)}) copy-start(f32[16,4,96,128]{3,2,1,0:T(8,128)} %p_ref.1) | copy-start | bytes 9437188
  1.9 1.1 copy-start.1
  3.0 1.1 copy-start.2
  4.0 0.7 copy-start.3
